TPU v7x, 32 devices: a whole 2x2x4 slice. The times are simulated.
32 devices in a mesh: sp: 2 (over x), ep: 16 (over z, y, core).
Axes of the slice: x: 2, y: 2, z: 4, core: 2. Of those that a mesh axis runs over, the one named last changes fastest.
Arguments:
- activations: bfloat16 [16, 8, 3584], P('ep', 'sp'), may hold values from -6 to 6
- out_grad: bfloat16 [16, 8, 3584], P('ep', 'sp'), may hold values from -6 to 6
- route_weights: bfloat16 [16, 8, 8], P('ep', 'sp'), may hold values from 0.019897461 to 0.5
- expert_ids: int32 [16, 8, 8], P('ep', 'sp'), may hold values from 0 to 15, all different within a row; in each aligned block of 8 rows (0 to 7, 8 to 15, ..., all dimensions but the last counted through in order) at most 6 rows name the same one
- w_gate: bfloat16 [16, 3584, 1024], P('ep', None, 'sp'), may hold values from -0.09375 to 0.09375
- w_up: bfloat16 [16, 3584, 1024], P('ep', None, 'sp'), may hold values from -0.09375 to 0.09375
- w_down: bfloat16 [16, 1024, 3584], P('ep', 'sp'), may hold values from -0.1875 to 0.1875
Outputs:
- input_grad: bfloat16 [16, 8, 3584], P('ep', 'sp')
- w_down_grad: float32 [16, 1024, 3584], P('ep', 'sp')
Inputs may be any that keep to these rules, and one draw needn't show every extreme that they name: `expert_ids`: each row names 8 different experts. In each aligned block of 8 rows (one token group, the first two dimensions taken together) no expert is named by more than 6 rows, a bound that some block reaches.
All inputs are finite; a program needn't handle non-finite values.
Results may differ from a plain program's by a relative error of at most 0.014.
Values may be sent and summed in bfloat16 or wider, within the bound.
No kernel may reach another device: no remote copies, remote signals or barrier semaphores. Data moves between devices by JAX's collectives and lax.ppermute only.
A program may use at most 64 MiB of HBM per device.

v0:
```python
import jax
import jax.numpy as jnp
from jax import lax
from jax.sharding import PartitionSpec as P

TOP = 8


def expert_rows(rows_in, rows_grad, gate_w, up_w, down_w):
    gate_pre = jnp.dot(rows_in, gate_w, preferred_element_type=jnp.float32)
    up_pre = jnp.dot(rows_in, up_w, preferred_element_type=jnp.float32)
    squash = jax.nn.sigmoid(gate_pre)
    swish = gate_pre * squash
    hidden = (swish * up_pre).astype(jnp.bfloat16)
    hidden_grad = lax.dot_general(
        rows_grad, down_w, (((1,), (1,)), ((), ())), preferred_element_type=jnp.float32
    )
    gate_grad = (hidden_grad * up_pre * squash * (1.0 + gate_pre * (1.0 - squash))).astype(
        jnp.bfloat16
    )
    up_grad = (hidden_grad * swish).astype(jnp.bfloat16)
    first = lax.dot_general(
        gate_grad, gate_w, (((1,), (1,)), ((), ())), preferred_element_type=jnp.float32
    )
    second = lax.dot_general(
        up_grad, up_w, (((1,), (1,)), ((), ())), preferred_element_type=jnp.float32
    )
    partial_rows = (first + second).astype(jnp.bfloat16)
    weight_grad = lax.dot_general(
        hidden, rows_grad, (((0,), (0,)), ((), ())), preferred_element_type=jnp.float32
    )
    return (partial_rows, weight_grad)


def per_device(activations, out_grad, route_weights, expert_ids, w_gate, w_up, w_down):
    n_expert = lax.axis_size("ep")
    n_group = lax.axis_size("sp")
    tok_dev = activations.shape[1]
    width = activations.shape[2]
    capacity = max(2, tok_dev * n_group * TOP * 3 // (2 * n_expert))
    group_ids = lax.all_gather(expert_ids, "sp", axis=1, tiled=True)
    group_in, group_grad, group_weight = (
        lax.all_gather(activations, "sp", axis=1, tiled=True),
        lax.all_gather(out_grad, "sp", axis=1, tiled=True),
        lax.all_gather(route_weights, "sp", axis=1, tiled=True),
    )
    send_width = group_in.shape[2]
    tok_grp = group_ids.shape[1]
    slot_expert = group_ids[0].reshape(-1)
    slot_token = jnp.arange(slot_expert.shape[0], dtype=jnp.int32) // TOP
    onehot = (slot_expert[:, None] == jnp.arange(n_expert, dtype=jnp.int32)[None, :]).astype(
        jnp.int32
    )
    before = jnp.cumsum(onehot, axis=0) - onehot
    rank = jnp.sum(before * onehot, axis=1)
    position = slot_expert * capacity + rank
    total_rows = n_expert * capacity
    token_in = group_in[0][slot_token]
    scaled = (
        group_weight[0].reshape(-1).astype(jnp.float32)[:, None]
        * group_grad[0][slot_token].astype(jnp.float32)
    ).astype(jnp.bfloat16)
    send_in = (
        jnp.zeros((total_rows, send_width), jnp.bfloat16)
        .at[position]
        .set(token_in)
        .reshape(n_expert, capacity, send_width)
    )
    send_grad = (
        jnp.zeros((total_rows, send_width), jnp.bfloat16)
        .at[position]
        .set(scaled)
        .reshape(n_expert, capacity, send_width)
    )
    recv_in, recv_grad = (
        lax.all_to_all(send_in, "ep", split_axis=0, concat_axis=0, tiled=True),
        lax.all_to_all(send_grad, "ep", split_axis=0, concat_axis=0, tiled=True),
    )
    flat_in = recv_in.reshape(total_rows, width)
    flat_grad = recv_grad.reshape(total_rows, width)
    gate_w = w_gate[0]
    up_w = w_up[0]
    down_w = w_down[0]
    partial_rows, weight_grad = expert_rows(flat_in, flat_grad, gate_w, up_w, down_w)
    partial_rows = partial_rows.reshape(n_expert, capacity, width)
    slot_owner = jnp.full((total_rows,), -1, jnp.int32).at[position].set(slot_token)
    owner_match = jnp.arange(tok_grp, dtype=jnp.int32)[:, None] == slot_owner[None, :]
    back_rows = lax.all_to_all(partial_rows, "ep", split_axis=0, concat_axis=0, tiled=True)
    token_sum = jnp.dot(
        owner_match.astype(jnp.bfloat16),
        back_rows.reshape(total_rows, width),
        preferred_element_type=jnp.float32,
    )
    own_sum = lax.psum_scatter(
        token_sum.astype(jnp.bfloat16), "sp", scatter_dimension=0, tiled=True
    )
    return (own_sum.reshape(1, tok_dev, width), weight_grad[None])


def solution(mesh):
    return jax.shard_map(
        per_device,
        mesh=mesh,
        in_specs=(
            P("ep", "sp", None),
            P("ep", "sp", None),
            P("ep", "sp", None),
            P("ep", "sp", None),
            P("ep", None, "sp"),
            P("ep", None, "sp"),
            P("ep", "sp", None),
        ),
        out_specs=(P("ep", "sp", None), P("ep", "sp", None)),
        check_vma=False,
    )
```

profile of v0, /device:TPU:16, one launch (start us, length us, event | category | flops | bytes accessed | tf_op | source)
XLA Modules:
  0.0 116.9 jit_solution(2344344698198534478)
XLA Ops:
  0.7 4.5 %all_gather.12 = s32[1,8,8]{2,0,1:T(1,128)S(1)} all-gather(s32[1,4,8]{2,0,1:T(1,128)} %bitcast.44), channel_id=1, replica_groups=mesh['sp'=2,'ep'=16] {'sp'}, dimensions={1}, use_global_device_ids=true | all-gather | bytes 384 | tf_op jit(solution)/shard_map/all_gather | solution.py:41
  6.9 0.8 copy.16
  7.7 4.8 %all_gather.15 = bf16[1,8,3584]{2,0,1:T(2,128)(2,1)S(1)} all-gather(bf16[1,4,3584]{2,0,1:T(2,128)(2,1)S(1)} %copy.16), channel_id=1, replica_groups=mesh['sp'=2,'ep'=16] {'sp'}, dimensions={1}, use_global_device_ids=true | all-gather | bytes 86016 | tf_op jit(solution)/shard_map/all_gather | solution.py:43
  12.6 2.8 %scatter_custom_fusion.2 = bf16[96,3584]{1,0:T(8,128)(2,1)S(1)} fusion(s32[64]{0:T(128)S(1)} %fusion.23, bf16[8,3584]{1,0:T(8,128)(2,1)S(1)} %bitcast.43, s32[1024]{0:T(1024)S(1)} %pad_clamp_fusion, bf16[]{:T(256)} %constant.34.clone.1), kind=kCustom, calls=%fused_computation.20 | custom fusion | bytes 688130 | tf_op jit(solution)/shard_map/scatter | solution.py:66
  15.4 1.2 reshape.107
  16.5 6.2 %all-to-all-start.1 = ((bf16[16,6,3584]{2,1,0:T(8,128)(2,1)}), bf16[16,6,3584]{2,1,0:T(8,128)(2,1)S(1)}, u32[]{:S(2)}, u32[]{:S(2)}) async-start(bf16[16,6,3584]{2,1,0:T(8,128)(2,1)} %reshape.107), calls=%async_computation.1 | async-start | bytes 1835008 | tf_op jit(solution)/shard_map/all_to_all | solution.py:76
  22.7 4.4 %all_gather.13 = bf16[1,8,8]{2,0,1:T(2,128)(2,1)S(1)} all-gather(bf16[1,4,8]{2,0,1:T(2,128)(2,1)S(1)} %copy.14), channel_id=1, replica_groups=mesh['sp'=2,'ep'=16] {'sp'}, dimensions={1}, use_global_device_ids=true | all-gather | bytes 192 | tf_op jit(solution)/shard_map/all_gather | solution.py:45
  27.2 4.8 %all_gather.14 = bf16[1,8,3584]{2,0,1:T(2,128)(2,1)S(1)} all-gather(bf16[1,4,3584]{2,0,1:T(2,128)(2,1)S(1)} %copy.15), channel_id=1, replica_groups=mesh['sp'=2,'ep'=16] {'sp'}, dimensions={1}, use_global_device_ids=true | all-gather | bytes 86016 | tf_op jit(solution)/shard_map/all_gather | solution.py:44
  32.1 2.9 %scatter_custom_fusion.1 = bf16[96,3584]{1,0:T(8,128)(2,1)S(1)} fusion(s32[64]{0:T(128)S(1)} %fusion.23, f32[64]{0:T(128)S(1)} %reshape.112, bf16[]{:T(256)} %constant.34.clone.1, bf16[8,3584]{1,0:T(8,128)(2,1)S(1)} %bitcast.42, s32[1024]{0:T(1024)S(1)} %pad_clamp_fusion), kind=kCustom, calls=%fused_computation.19 | custom fusion | flops 688128 | bytes 750082 | tf_op jit(solution)/shard_map/scatter | solution.py:72
  35.0 1.2 reshape.105
  36.1 8.9 %all-to-all-done.1 = bf16[16,6,3584]{2,1,0:T(8,128)(2,1)S(1)} async-done(((bf16[16,6,3584]{2,1,0:T(8,128)(2,1)}), bf16[16,6,3584]{2,1,0:T(8,128)(2,1)S(1)}, u32[]{:S(2)}, u32[]{:S(2)}) %all-to-all-start.1) | async-done | bytes 688160 | tf_op jit(solution)/shard_map/all_to_all | solution.py:76
  45.0 4.5 %all-to-all-start = ((bf16[16,6,3584]{2,1,0:T(8,128)(2,1)}), bf16[16,6,3584]{2,1,0:T(8,128)(2,1)S(1)}, u32[]{:S(2)}, u32[]{:S(2)}) async-start(bf16[16,6,3584]{2,1,0:T(8,128)(2,1)} %reshape.105), calls=%async_computation | async-start | bytes 1835008 | tf_op jit(solution)/shard_map/all_to_all | solution.py:77
  49.8 2.9 %fusion.3 = f32[96,512]{1,0:T(8,128)S(1)} fusion(bf16[96,3584]{1,0:T(8,128)(2,1)S(1)} %reshape.108, bf16[1,3584,512]{2,1,0:T(8,128)(2,1)} %param.11), kind=kOutput, calls=%fused_computation.11 | convolution fusion | flops 352321536 | bytes 4554752 | tf_op jit(solution)/shard_map/dot_general | solution.py:10
  53.7 18.2 %all-to-all-done = bf16[16,6,3584]{2,1,0:T(8,128)(2,1)S(1)} async-done(((bf16[16,6,3584]{2,1,0:T(8,128)(2,1)}), bf16[16,6,3584]{2,1,0:T(8,128)(2,1)S(1)}, u32[]{:S(2)}, u32[]{:S(2)}) %all-to-all-start) | async-done | bytes 688160 | tf_op jit(solution)/shard_map/all_to_all | solution.py:77
  72.2 3.4 %fusion.8 = f32[96,512]{1,0:T(8,128)S(1)} fusion(bf16[96,3584]{1,0:T(8,128)(2,1)S(1)} %reshape.106, bf16[1,512,3584]{2,1,0:T(8,128)(2,1)} %param.13), kind=kOutput, calls=%fused_computation.16 | convolution fusion | flops 352321536 | bytes 4554752 | tf_op jit(solution)/shard_map/dot_general | solution.py:15
  75.6 1.2 %fusion.1 = f32[96,3584]{1,0:T(8,128)S(1)} fusion(bf16[1,3584,512]{2,1,0:T(8,128)(2,1)S(1)} %copy-done, f32[96,512]{1,0:T(8,128)S(1)} %fusion.3, f32[96,512]{1,0:T(8,128)S(1)} %fusion.8, f32[96,512]{1,0:T(8,128)S(1)} %fusion.6), kind=kOutput, calls=%fused_computation.9 | convolution fusion | flops 352813056 | bytes 5636096 | tf_op jit(solution)/shard_map/dot_general | solution.py:22
  76.8 0.8 copy-done.2
  77.6 1.2 %fusion = bf16[96,3584]{1,0:T(8,128)(2,1)S(1)} fusion(f32[96,3584]{1,0:T(8,128)S(1)} %fusion.1, bf16[1,3584,512]{2,1,0:T(8,128)(2,1)S(1)} %copy-done.2, f32[96,512]{1,0:T(8,128)S(1)} %fusion.8, f32[96,512]{1,0:T(8,128)S(1)} %fusion.3), kind=kOutput, calls=%fused_computation.7 | convolution fusion | flops 353304576 | bytes 6127616 | tf_op jit(solution)/shard_map/dot_general | solution.py:25
  78.9 1.2 reshape.109
  80.0 4.5 %all-to-all-start.2 = ((bf16[16,6,3584]{2,1,0:T(8,128)(2,1)}), bf16[16,6,3584]{2,1,0:T(8,128)(2,1)S(1)}, u32[]{:S(2)}, u32[]{:S(2)}) async-start(bf16[16,6,3584]{2,1,0:T(8,128)(2,1)} %reshape.109), calls=%async_computation.2 | async-start | bytes 1835008 | tf_op jit(solution)/shard_map/all_to_all | solution.py:88
  85.8 0.8 scatter_custom_fusion
  86.6 4.2 %convolution_bitcast_fusion = f32[1,512,3584]{2,1,0:T(8,128)} fusion(bf16[96,3584]{1,0:T(8,128)(2,1)S(1)} %reshape.106, f32[96,512]{1,0:T(8,128)S(1)} %fusion.6, f32[96,512]{1,0:T(8,128)S(1)} %fusion.3), kind=kOutput, calls=%fused_computation.5 | convolution fusion | flops 352616448 | bytes 8421376 | tf_op jit(solution)/shard_map/dot_general | solution.py:29
  90.8 16.1 %all-to-all-done.2 = bf16[16,6,3584]{2,1,0:T(8,128)(2,1)S(1)} async-done(((bf16[16,6,3584]{2,1,0:T(8,128)(2,1)}), bf16[16,6,3584]{2,1,0:T(8,128)(2,1)S(1)}, u32[]{:S(2)}, u32[]{:S(2)}) %all-to-all-start.2) | async-done | bytes 688160 | tf_op jit(solution)/shard_map/all_to_all | solution.py:88
  107.3 9.0 %all-reduce = bf16[8,3584]{1,0:T(8,128)(2,1)S(1)} all-reduce(bf16[8,3584]{1,0:T(8,128)(2,1)S(1)} %convolution_convert_fusion), channel_id=2, replica_groups=mesh['sp'=2,'ep'=16] {'sp'}, use_global_device_ids=true, to_apply=%region_5.6.clone | all-reduce | flops 28672 | bytes 114688
  (35 shorter events, 4.9 us)
Async XLA Ops:
  0.6 22.1 %copy-start.4 = (bf16[1,4,8]{2,1,0:T(4,128)(2,1)S(1)}, bf16[1,4,8]{2,1,0:T(4,128)(2,1)}, u32[]{:S(2)}) copy-start(bf16[1,4,8]{2,1,0:T(4,128)(2,1)} %param.9) | copy-start | bytes 196
  0.6 26.6 %copy-start.3 = (bf16[1,4,3584]{2,1,0:T(4,128)(2,1)S(1)}, bf16[1,4,3584]{2,1,0:T(4,128)(2,1)}, u32[]{:S(2)}) copy-start(bf16[1,4,3584]{2,1,0:T(4,128)(2,1)} %param.8) | copy-start | bytes 86020
  16.5 28.5 %all-to-all-start.1 = ((bf16[16,6,3584]{2,1,0:T(8,128)(2,1)}), bf16[16,6,3584]{2,1,0:T(8,128)(2,1)S(1)}, u32[]{:S(2)}, u32[]{:S(2)}) async-start(bf16[16,6,3584]{2,1,0:T(8,128)(2,1)} %reshape.107), calls=%async_computation.1 | async-start | bytes 1835008 | tf_op jit(solution)/shard_map/all_to_all | solution.py:76
  45.0 26.9 %all-to-all-start = ((bf16[16,6,3584]{2,1,0:T(8,128)(2,1)}), bf16[16,6,3584]{2,1,0:T(8,128)(2,1)S(1)}, u32[]{:S(2)}, u32[]{:S(2)}) async-start(bf16[16,6,3584]{2,1,0:T(8,128)(2,1)} %reshape.105), calls=%async_computation | async-start | bytes 1835008 | tf_op jit(solution)/shard_map/all_to_all | solution.py:77
  49.8 3.1 %copy-start.1 = (bf16[1,3584,512]{2,1,0:T(8,128)(2,1)S(1)}, bf16[1,3584,512]{2,1,0:T(8,128)(2,1)}, u32[]{:S(2)}) copy-start(bf16[1,3584,512]{2,1,0:T(8,128)(2,1)} %param.12) | copy-start | bytes 11010052
  72.1 3.4 %copy-start = (bf16[1,3584,512]{2,1,0:T(8,128)(2,1)S(1)}, bf16[1,3584,512]{2,1,0:T(8,128)(2,1)}, u32[]{:S(2)}) copy-start(bf16[1,3584,512]{2,1,0:T(8,128)(2,1)} %param.11) | copy-start | bytes 11010052
  75.6 2.0 %copy-start.2 = (bf16[1,3584,512]{2,1,0:T(8,128)(2,1)S(1)}, bf16[1,3584,512]{2,1,0:T(8,128)(2,1)}, u32[]{:S(2)}) copy-start(bf16[1,3584,512]{2,1,0:T(8,128)(2,1)} %param.12) | copy-start | bytes 11010052
  77.6 7.0 %copy-start.5 = (u32[32]{0:T(128)S(1)}, u32[32]{0:T(128)}, u32[]{:S(2)}) copy-start(u32[32]{0:T(128)} %constant.46) | copy-start | bytes 388
  80.0 26.9 %all-to-all-start.2 = ((bf16[16,6,3584]{2,1,0:T(8,128)(2,1)}), bf16[16,6,3584]{2,1,0:T(8,128)(2,1)S(1)}, u32[]{:S(2)}, u32[]{:S(2)}) async-start(bf16[16,6,3584]{2,1,0:T(8,128)(2,1)} %reshape.109), calls=%async_computation.2 | async-start | bytes 1835008 | tf_op jit(solution)/shard_map/all_to_all | solution.py:88
where the time goes:
time: 118 us; the launch traced here: 117 us
  waiting for transfers between devices  43.3 us (37%)
  blocking collectives  27.5 us (23%)
  starting transfers between devices  15.3 us (13%)
  matrix products  13.9 us (12%)
  local copies, waits for them, and re-layouts  11.6 us (10%)
  other arithmetic  3.92 us (3%)
  between operations  1.49 us (1%)
    all_to_all x1, waiting for transfers between devices, per_device(): lax.all_to_all(send_grad, 'ep', split_axis=0, concat_axis=0, tiled=True)  18.2 us
    all_to_all x1, waiting for transfers between devices, per_device(): lax.all_to_all(partial_rows, 'ep', split_axis=0, concat_axis=0, tiled=True)  16.1 us
    unnamed x1, blocking collectives  8.96 us
    all_to_all x1, waiting for transfers between devices, per_device(): lax.all_to_all(send_in, 'ep', split_axis=0, concat_axis=0, tiled=True)  8.92 us
    all_to_all x1, starting transfers between devices, per_device(): lax.all_to_all(send_in, 'ep', split_axis=0, concat_axis=0, tiled=True)  6.18 us
    all_gather x1, blocking collectives, per_device(): lax.all_gather(activations, 'sp', axis=1, tiled=True)  4.85 us
    all_gather x1, blocking collectives, per_device(): lax.all_gather(out_grad, 'sp', axis=1, tiled=True)  4.85 us
    all_to_all x1, starting transfers between devices, per_device(): lax.all_to_all(send_grad, 'ep', split_axis=0, concat_axis=0, tiled=True)  4.53 us
  transfers between devices with their start and end apart: 3, of which 3 were waited for; matrix products, arithmetic and copies ran while one was open for 12% of the time, Pallas kernels for 0%

commit v1 on v0

--- a/solution.py
+++ b/solution.py
@@ -4,6 +4,18 @@
 from jax.sharding import PartitionSpec as P
 
 TOP = 8
+
+
+def exchange_directly(x, axis, split, join):
+    ways, here = (lax.axis_size(axis), lax.axis_index(axis))
+    width = x.shape[split] // ways
+    turned = jnp.roll(x, -here * width, axis=split)
+    got = [lax.slice_in_dim(turned, 0, width, axis=split)]
+    for far in range(1, ways):
+        sent = lax.slice_in_dim(turned, far * width, (far + 1) * width, axis=split)
+        got.append(lax.ppermute(sent, axis, [(d, (d + far) % ways) for d in range(ways)]))
+    line = jnp.concatenate(got[::-1], axis=join)
+    return jnp.roll(line, (here + 1) * got[0].shape[join], axis=join)
 
 
 def expert_rows(rows_in, rows_grad, gate_w, up_w, down_w):
@@ -74,7 +86,7 @@
     )
     recv_in, recv_grad = (
         lax.all_to_all(send_in, "ep", split_axis=0, concat_axis=0, tiled=True),
-        lax.all_to_all(send_grad, "ep", split_axis=0, concat_axis=0, tiled=True),
+        exchange_directly(send_grad, "ep", 0, 0),
     )
     flat_in = recv_in.reshape(total_rows, width)
     flat_grad = recv_grad.reshape(total_rows, width)

time: 118 us -> 161 us (1.36)
  waiting for transfers between devices: 43.3 us -> 66.9 us
  starting transfers between devices: 15.3 us -> 32.6 us
  matrix products: 13.9 us -> 15.8 us
    ppermute x0 -> x15, waiting for transfers between devices: none -> 50.8 us  [exchange_directly(): lax.ppermute(sent, axis, [(d, (d + far) % ways) for d in range(ways)])]
    ppermute x0 -> x15, starting transfers between devices: none -> 19.4 us  [exchange_directly(): lax.ppermute(sent, axis, [(d, (d + far) % ways) for d in range(ways)])]
    all_to_all x1 -> x0, waiting for transfers between devices: 18.2 us -> none  [per_device(): lax.all_to_all(send_grad, 'ep', split_axis=0, concat_axis=0, tiled=True)]
    all_to_all x1, waiting for transfers between devices: 8.92 us -> 0.01 us  [per_device(): lax.all_to_all(send_in, 'ep', split_axis=0, concat_axis=0, tiled=True)]
    all_to_all x1 -> x0, starting transfers between devices: 4.53 us -> none  [per_device(): lax.all_to_all(send_grad, 'ep', split_axis=0, concat_axis=0, tiled=True)]
    all_to_all x1, starting transfers between devices: 4.53 us -> 7.01 us  [per_device(): lax.all_to_all(partial_rows, 'ep', split_axis=0, concat_axis=0, tiled=True)]
    dot_general x1, matrix products: 0.71 us -> 2.76 us  [expert_rows(): up_pre = jnp.dot(rows_in, up_w, preferred_element_type=jnp.float32)]
  transfers between devices with their start and end apart: 3 -> 17, of which waited for: 3 -> 11; matrix products, arithmetic and copies ran while one was open for 12% -> 8% of each run, Pallas kernels for 0% -> 0%
where the time goes in v1:
time: 161 us
  waiting for transfers between devices  66.9 us (42%)
  starting transfers between devices  32.6 us (20%)
  blocking collectives  27.6 us (17%)
  matrix products  15.8 us (10%)
  local copies, waits for them, and re-layouts  11.2 us (7%)
  other arithmetic  4.85 us (3%)
  between operations  1.62 us (1%)
    ppermute x15, waiting for transfers between devices, exchange_directly(): lax.ppermute(sent, axis, [(d, (d + far) % ways) for d in range(ways)])  50.8 us
    ppermute x15, starting transfers between devices, exchange_directly(): lax.ppermute(sent, axis, [(d, (d + far) % ways) for d in range(ways)])  19.4 us
    all_to_all x1, waiting for transfers between devices, per_device(): lax.all_to_all(partial_rows, 'ep', split_axis=0, concat_axis=0, tiled=True)  16.1 us
    unnamed x1, blocking collectives  8.98 us
    all_to_all x1, starting transfers between devices, per_device(): lax.all_to_all(partial_rows, 'ep', split_axis=0, concat_axis=0, tiled=True)  7.01 us
    all_to_all x1, starting transfers between devices, per_device(): lax.all_to_all(send_in, 'ep', split_axis=0, concat_axis=0, tiled=True)  6.18 us
    all_gather x1, blocking collectives, per_device(): lax.all_gather(activations, 'sp', axis=1, tiled=True)  4.97 us
    all_gather x1, blocking collectives, per_device(): lax.all_gather(out_grad, 'sp', axis=1, tiled=True)  4.85 us
  transfers between devices with their start and end apart: 17, of which 11 were waited for; matrix products, arithmetic and copies ran while one was open for 8% of the time, Pallas kernels for 0%

profile of v1, /device:TPU:16, one launch (start us, length us, event | category | flops | bytes accessed | tf_op | source)
XLA Modules:
  0.0 160.6 jit_solution(8102471762609889050)
XLA Ops:
  1.3 4.4 %all_gather.13 = bf16[1,8,8]{2,0,1:T(2,128)(2,1)S(1)} all-gather(bf16[1,4,8]{2,0,1:T(2,128)(2,1)S(1)} %copy.14), channel_id=1, replica_groups=mesh['sp'=2,'ep'=16] {'sp'}, dimensions={1}, use_global_device_ids=true | all-gather | bytes 192 | tf_op jit(solution)/shard_map/all_gather | solution.py:57
  5.8 4.5 %all_gather.12 = s32[1,8,8]{2,0,1:T(1,128)S(1)} all-gather(s32[1,4,8]{2,0,1:T(1,128)} %bitcast.44), channel_id=1, replica_groups=mesh['sp'=2,'ep'=16] {'sp'}, dimensions={1}, use_global_device_ids=true | all-gather | bytes 384 | tf_op jit(solution)/shard_map/all_gather | solution.py:53
  12.8 4.8 %all_gather.14 = bf16[1,8,3584]{2,0,1:T(2,128)(2,1)S(1)} all-gather(bf16[1,4,3584]{2,0,1:T(2,128)(2,1)S(1)} %copy.15), channel_id=1, replica_groups=mesh['sp'=2,'ep'=16] {'sp'}, dimensions={1}, use_global_device_ids=true | all-gather | bytes 86016 | tf_op jit(solution)/shard_map/all_gather | solution.py:56
  17.7 2.9 %scatter_custom_fusion.1 = bf16[96,3584]{1,0:T(8,128)(2,1)S(1)} fusion(s32[64]{0:T(128)S(1)} %get-tuple-element.21, f32[64]{0:T(128)S(1)} %reshape.112, bf16[]{:T(256)} %constant.55.clone.1, bf16[8,3584]{1,0:T(8,128)(2,1)S(1)} %bitcast.42, s32[1024]{0:T(1024)S(1)} %pad_clamp_fusion), kind=kCustom, calls=%fused_computation.25 | custom fusion | flops 688128 | bytes 750082 | tf_op jit(solution)/shard_map/scatter | solution.py:84
  21.5 5.0 %all_gather.15 = bf16[1,8,3584]{2,0,1:T(2,128)(2,1)S(1)} all-gather(bf16[1,4,3584]{2,0,1:T(2,128)(2,1)S(1)} %copy.16), channel_id=1, replica_groups=mesh['sp'=2,'ep'=16] {'sp'}, dimensions={1}, use_global_device_ids=true | all-gather | bytes 86016 | tf_op jit(solution)/shard_map/all_gather | solution.py:55
  26.4 2.8 %scatter_custom_fusion.2 = bf16[96,3584]{1,0:T(8,128)(2,1)S(1)} fusion(s32[64]{0:T(128)S(1)} %get-tuple-element.21, bf16[8,3584]{1,0:T(8,128)(2,1)S(1)} %bitcast.43, s32[1024]{0:T(1024)S(1)} %pad_clamp_fusion, bf16[]{:T(256)} %constant.55.clone.1), kind=kCustom, calls=%fused_computation.26 | custom fusion | bytes 688130 | tf_op jit(solution)/shard_map/scatter | solution.py:78
  30.4 6.2 %all-to-all-start = ((bf16[16,6,3584]{2,1,0:T(8,128)(2,1)}), bf16[16,6,3584]{2,1,0:T(8,128)(2,1)S(1)}, u32[]{:S(2)}, u32[]{:S(2)}) async-start(bf16[16,6,3584]{2,1,0:T(8,128)(2,1)} %reshape.107), calls=%async_computation | async-start | bytes 1835008 | tf_op jit(solution)/shard_map/all_to_all | solution.py:88
  42.2 17.9 %collective-permute-done.1 = bf16[1,6,3584]{2,1,0:T(8,128)(2,1)S(1)} collective-permute-done((bf16[1,6,3584]{2,1,0:T(8,128)(2,1)S(1)}, bf16[1,6,3584]{2,1,0:T(8,128)(2,1)S(1)}, u32[]{:S(2)}, u32[]{:S(2)}) %collective-permute-start.1) | collective-permute-done | bytes 43040 | tf_op jit(solution)/shard_map/ppermute | solution.py:16
  60.1 3.6 %collective-permute-done.2 = bf16[1,6,3584]{2,1,0:T(8,128)(2,1)S(1)} collective-permute-done((bf16[1,6,3584]{2,1,0:T(8,128)(2,1)S(1)}, bf16[1,6,3584]{2,1,0:T(8,128)(2,1)S(1)}, u32[]{:S(2)}, u32[]{:S(2)}) %collective-permute-start.2) | collective-permute-done | bytes 43040 | tf_op jit(solution)/shard_map/ppermute | solution.py:16
  65.1 3.3 %collective-permute-done.3 = bf16[1,6,3584]{2,1,0:T(8,128)(2,1)S(1)} collective-permute-done((bf16[1,6,3584]{2,1,0:T(8,128)(2,1)S(1)}, bf16[1,6,3584]{2,1,0:T(8,128)(2,1)S(1)}, u32[]{:S(2)}, u32[]{:S(2)}) %collective-permute-start.3) | collective-permute-done | bytes 43040 | tf_op jit(solution)/shard_map/ppermute | solution.py:16
  71.9 3.3 %collective-permute-start.5 = (bf16[1,6,3584]{2,1,0:T(8,128)(2,1)S(1)}, bf16[1,6,3584]{2,1,0:T(8,128)(2,1)S(1)}, u32[]{:S(2)}, u32[]{:S(2)}) collective-permute-start(bf16[1,6,3584]{2,1,0:T(8,128)(2,1)S(1)} %get-tuple-element.14), channel_id=1, source_target_pairs={{0,10},{1,11},{2,12},{3,13},{4,14},{5,15},{6,0},{7,1},{8,2},{9,3},... | collective-permute-start | bytes 129032 | tf_op jit(solution)/shard_map/ppermute | solution.py:16
  75.3 2.8 %collective-permute-done.5 = bf16[1,6,3584]{2,1,0:T(8,128)(2,1)S(1)} collective-permute-done((bf16[1,6,3584]{2,1,0:T(8,128)(2,1)S(1)}, bf16[1,6,3584]{2,1,0:T(8,128)(2,1)S(1)}, u32[]{:S(2)}, u32[]{:S(2)}) %collective-permute-start.5) | collective-permute-done | bytes 43040 | tf_op jit(solution)/shard_map/ppermute | solution.py:16
  79.5 4.1 %collective-permute-done.6 = bf16[1,6,3584]{2,1,0:T(8,128)(2,1)S(1)} collective-permute-done((bf16[1,6,3584]{2,1,0:T(8,128)(2,1)S(1)}, bf16[1,6,3584]{2,1,0:T(8,128)(2,1)S(1)}, u32[]{:S(2)}, u32[]{:S(2)}) %collective-permute-start.6) | collective-permute-done | bytes 43040 | tf_op jit(solution)/shard_map/ppermute | solution.py:16
  84.2 4.5 %collective-permute-done.7 = bf16[1,6,3584]{2,1,0:T(8,128)(2,1)S(1)} collective-permute-done((bf16[1,6,3584]{2,1,0:T(8,128)(2,1)S(1)}, bf16[1,6,3584]{2,1,0:T(8,128)(2,1)S(1)}, u32[]{:S(2)}, u32[]{:S(2)}) %collective-permute-start.7) | collective-permute-done | bytes 43040 | tf_op jit(solution)/shard_map/ppermute | solution.py:16
  90.1 3.5 %collective-permute-done.8 = bf16[1,6,3584]{2,1,0:T(8,128)(2,1)S(1)} collective-permute-done((bf16[1,6,3584]{2,1,0:T(8,128)(2,1)S(1)}, bf16[1,6,3584]{2,1,0:T(8,128)(2,1)S(1)}, u32[]{:S(2)}, u32[]{:S(2)}) %collective-permute-start.8) | collective-permute-done | bytes 43040 | tf_op jit(solution)/shard_map/ppermute | solution.py:16
  93.6 4.4 %collective-permute-start.9 = (bf16[1,6,3584]{2,1,0:T(8,128)(2,1)S(1)}, bf16[1,6,3584]{2,1,0:T(8,128)(2,1)S(1)}, u32[]{:S(2)}, u32[]{:S(2)}) collective-permute-start(bf16[1,6,3584]{2,1,0:T(8,128)(2,1)S(1)} %get-tuple-element.10), channel_id=1, source_target_pairs={{0,6},{1,7},{2,8},{3,9},{4,10},{5,11},{6,12},{7,13},{8,14},{9,15},... | collective-permute-start | bytes 129032 | tf_op jit(solution)/shard_map/ppermute | solution.py:16
  98.0 3.4 %collective-permute-done.9 = bf16[1,6,3584]{2,1,0:T(8,128)(2,1)S(1)} collective-permute-done((bf16[1,6,3584]{2,1,0:T(8,128)(2,1)S(1)}, bf16[1,6,3584]{2,1,0:T(8,128)(2,1)S(1)}, u32[]{:S(2)}, u32[]{:S(2)}) %collective-permute-start.9) | collective-permute-done | bytes 43040 | tf_op jit(solution)/shard_map/ppermute | solution.py:16
  101.4 5.4 %collective-permute-done.10 = bf16[1,6,3584]{2,1,0:T(8,128)(2,1)S(1)} collective-permute-done((bf16[1,6,3584]{2,1,0:T(8,128)(2,1)S(1)}, bf16[1,6,3584]{2,1,0:T(8,128)(2,1)S(1)}, u32[]{:S(2)}, u32[]{:S(2)}) %collective-permute-start.10) | collective-permute-done | bytes 43040 | tf_op jit(solution)/shard_map/ppermute | solution.py:16
  107.6 3.3 %fusion.8 = f32[96,512]{1,0:T(8,128)S(1)} fusion(bf16[96,3584]{1,0:T(8,128)(2,1)S(1)} %reshape.106, bf16[1,512,3584]{2,1,0:T(8,128)(2,1)} %param.15), kind=kOutput, calls=%fused_computation.16 | convolution fusion | flops 352321536 | bytes 4554752 | tf_op jit(solution)/shard_map/dot_general | solution.py:27
  111.1 2.9 %fusion.3 = f32[96,512]{1,0:T(8,128)S(1)} fusion(bf16[96,3584]{1,0:T(8,128)(2,1)S(1)} %reshape.108, bf16[1,3584,512]{2,1,0:T(8,128)(2,1)} %param.13), kind=kOutput, calls=%fused_computation.11 | convolution fusion | flops 352321536 | bytes 4554752 | tf_op jit(solution)/shard_map/dot_general | solution.py:22
  121.2 7.0 %all-to-all-start.1 = ((bf16[16,6,3584]{2,1,0:T(8,128)(2,1)}), bf16[16,6,3584]{2,1,0:T(8,128)(2,1)S(1)}, u32[]{:S(2)}, u32[]{:S(2)}) async-start(bf16[16,6,3584]{2,1,0:T(8,128)(2,1)} %reshape.109), calls=%async_computation.1 | async-start | bytes 1835008 | tf_op jit(solution)/shard_map/all_to_all | solution.py:100
  130.3 4.2 %convolution_bitcast_fusion = f32[1,512,3584]{2,1,0:T(8,128)} fusion(bf16[96,3584]{1,0:T(8,128)(2,1)S(1)} %reshape.106, f32[96,512]{1,0:T(8,128)S(1)} %fusion.6, f32[96,512]{1,0:T(8,128)S(1)} %fusion.3), kind=kOutput, calls=%fused_computation.5 | convolution fusion | flops 352616448 | bytes 8421376 | tf_op jit(solution)/shard_map/dot_general | solution.py:41
  134.5 16.1 %all-to-all-done.1 = bf16[16,6,3584]{2,1,0:T(8,128)(2,1)S(1)} async-done(((bf16[16,6,3584]{2,1,0:T(8,128)(2,1)}), bf16[16,6,3584]{2,1,0:T(8,128)(2,1)S(1)}, u32[]{:S(2)}, u32[]{:S(2)}) %all-to-all-start.1) | async-done | bytes 688160 | tf_op jit(solution)/shard_map/all_to_all | solution.py:100
  151.0 9.0 %all-reduce = bf16[8,3584]{1,0:T(8,128)(2,1)S(1)} all-reduce(bf16[8,3584]{1,0:T(8,128)(2,1)S(1)} %convolution_convert_fusion), channel_id=2, replica_groups=mesh['sp'=2,'ep'=16] {'sp'}, use_global_device_ids=true, to_apply=%region_5.7.clone | all-reduce | flops 28672 | bytes 114688
  (77 shorter events, 29.9 us)
Async XLA Ops:
  0.6 20.8 %copy-start.2 = (bf16[1,4,3584]{2,1,0:T(4,128)(2,1)S(1)}, bf16[1,4,3584]{2,1,0:T(4,128)(2,1)}, u32[]{:S(2)}) copy-start(bf16[1,4,3584]{2,1,0:T(4,128)(2,1)} %param.9) | copy-start | bytes 86020
  21.3 19.6 %collective-permute-start = (bf16[1,6,3584]{2,1,0:T(8,128)(2,1)S(1)}, bf16[1,6,3584]{2,1,0:T(8,128)(2,1)S(1)}, u32[]{:S(2)}, u32[]{:S(2)}) collective-permute-start(bf16[1,6,3584]{2,1,0:T(8,128)(2,1)S(1)} %get-tuple-element.19), channel_id=1, source_target_pairs={{0,15},{1,0},{2,1},{3,2},{4,3},{5,4},{6,5},{7,6},{8,7},{9,8},{10,9... | collective-permute-start | bytes 129032 | tf_op jit(solution)/shard_map/ppermute | solution.py:16
  30.4 80.5 %all-to-all-start = ((bf16[16,6,3584]{2,1,0:T(8,128)(2,1)}), bf16[16,6,3584]{2,1,0:T(8,128)(2,1)S(1)}, u32[]{:S(2)}, u32[]{:S(2)}) async-start(bf16[16,6,3584]{2,1,0:T(8,128)(2,1)} %reshape.107), calls=%async_computation | async-start | bytes 1835008 | tf_op jit(solution)/shard_map/all_to_all | solution.py:88
  36.6 70.3 %collective-permute-start.14 = (bf16[1,6,3584]{2,1,0:T(8,128)(2,1)S(1)}, bf16[1,6,3584]{2,1,0:T(8,128)(2,1)S(1)}, u32[]{:S(2)}, u32[]{:S(2)}) collective-permute-start(bf16[1,6,3584]{2,1,0:T(8,128)(2,1)S(1)} %get-tuple-element.5), channel_id=1, source_target_pairs={{0,1},{1,2},{2,3},{3,4},{4,5},{5,6},{6,7},{7,8},{8,9},{9,10},{10,1... | collective-permute-start | bytes 129032 | tf_op jit(solution)/shard_map/ppermute | solution.py:16
  36.7 70.1 %collective-permute-start.13 = (bf16[1,6,3584]{2,1,0:T(8,128)(2,1)S(1)}, bf16[1,6,3584]{2,1,0:T(8,128)(2,1)S(1)}, u32[]{:S(2)}, u32[]{:S(2)}) collective-permute-start(bf16[1,6,3584]{2,1,0:T(8,128)(2,1)S(1)} %get-tuple-element.6), channel_id=1, source_target_pairs={{0,2},{1,3},{2,4},{3,5},{4,6},{5,7},{6,8},{7,9},{8,10},{9,11},{10,... | collective-permute-start | bytes 129032 | tf_op jit(solution)/shard_map/ppermute | solution.py:16
  38.2 68.6 %collective-permute-start.12 = (bf16[1,6,3584]{2,1,0:T(8,128)(2,1)S(1)}, bf16[1,6,3584]{2,1,0:T(8,128)(2,1)S(1)}, u32[]{:S(2)}, u32[]{:S(2)}) collective-permute-start(bf16[1,6,3584]{2,1,0:T(8,128)(2,1)S(1)} %get-tuple-element.7), channel_id=1, source_target_pairs={{0,3},{1,4},{2,5},{3,6},{4,7},{5,8},{6,9},{7,10},{8,11},{9,12},{10... | collective-permute-start | bytes 129032 | tf_op jit(solution)/shard_map/ppermute | solution.py:16
  40.4 66.3 %collective-permute-start.11 = (bf16[1,6,3584]{2,1,0:T(8,128)(2,1)S(1)}, bf16[1,6,3584]{2,1,0:T(8,128)(2,1)S(1)}, u32[]{:S(2)}, u32[]{:S(2)}) collective-permute-start(bf16[1,6,3584]{2,1,0:T(8,128)(2,1)S(1)} %get-tuple-element.8), channel_id=1, source_target_pairs={{0,4},{1,5},{2,6},{3,7},{4,8},{5,9},{6,10},{7,11},{8,12},{9,13},{1... | collective-permute-start | bytes 129032 | tf_op jit(solution)/shard_map/ppermute | solution.py:16
  41.0 19.1 %collective-permute-start.1 = (bf16[1,6,3584]{2,1,0:T(8,128)(2,1)S(1)}, bf16[1,6,3584]{2,1,0:T(8,128)(2,1)S(1)}, u32[]{:S(2)}, u32[]{:S(2)}) collective-permute-start(bf16[1,6,3584]{2,1,0:T(8,128)(2,1)S(1)} %get-tuple-element.18), channel_id=1, source_target_pairs={{0,14},{1,15},{2,0},{3,1},{4,2},{5,3},{6,4},{7,5},{8,6},{9,7},{10,... | collective-permute-start | bytes 129032 | tf_op jit(solution)/shard_map/ppermute | solution.py:16
  60.1 3.6 %collective-permute-start.2 = (bf16[1,6,3584]{2,1,0:T(8,128)(2,1)S(1)}, bf16[1,6,3584]{2,1,0:T(8,128)(2,1)S(1)}, u32[]{:S(2)}, u32[]{:S(2)}) collective-permute-start(bf16[1,6,3584]{2,1,0:T(8,128)(2,1)S(1)} %get-tuple-element.17), channel_id=1, source_target_pairs={{0,13},{1,14},{2,15},{3,0},{4,1},{5,2},{6,3},{7,4},{8,5},{9,6},{10... | collective-permute-start | bytes 129032 | tf_op jit(solution)/shard_map/ppermute | solution.py:16
  63.7 4.6 %collective-permute-start.3 = (bf16[1,6,3584]{2,1,0:T(8,128)(2,1)S(1)}, bf16[1,6,3584]{2,1,0:T(8,128)(2,1)S(1)}, u32[]{:S(2)}, u32[]{:S(2)}) collective-permute-start(bf16[1,6,3584]{2,1,0:T(8,128)(2,1)S(1)} %get-tuple-element.16), channel_id=1, source_target_pairs={{0,12},{1,13},{2,14},{3,15},{4,0},{5,1},{6,2},{7,3},{8,4},{9,5},{1... | collective-permute-start | bytes 129032 | tf_op jit(solution)/shard_map/ppermute | solution.py:16
  68.3 3.6 %collective-permute-start.4 = (bf16[1,6,3584]{2,1,0:T(8,128)(2,1)S(1)}, bf16[1,6,3584]{2,1,0:T(8,128)(2,1)S(1)}, u32[]{:S(2)}, u32[]{:S(2)}) collective-permute-start(bf16[1,6,3584]{2,1,0:T(8,128)(2,1)S(1)} %get-tuple-element.15), channel_id=1, source_target_pairs={{0,11},{1,12},{2,13},{3,14},{4,15},{5,0},{6,1},{7,2},{8,3},{9,4},{... | collective-permute-start | bytes 129032 | tf_op jit(solution)/shard_map/ppermute | solution.py:16
  71.9 6.1 %collective-permute-start.5 = (bf16[1,6,3584]{2,1,0:T(8,128)(2,1)S(1)}, bf16[1,6,3584]{2,1,0:T(8,128)(2,1)S(1)}, u32[]{:S(2)}, u32[]{:S(2)}) collective-permute-start(bf16[1,6,3584]{2,1,0:T(8,128)(2,1)S(1)} %get-tuple-element.14), channel_id=1, source_target_pairs={{0,10},{1,11},{2,12},{3,13},{4,14},{5,15},{6,0},{7,1},{8,2},{9,3},... | collective-permute-start | bytes 129032 | tf_op jit(solution)/shard_map/ppermute | solution.py:16
  78.1 5.5 %collective-permute-start.6 = (bf16[1,6,3584]{2,1,0:T(8,128)(2,1)S(1)}, bf16[1,6,3584]{2,1,0:T(8,128)(2,1)S(1)}, u32[]{:S(2)}, u32[]{:S(2)}) collective-permute-start(bf16[1,6,3584]{2,1,0:T(8,128)(2,1)S(1)} %get-tuple-element.13), channel_id=1, source_target_pairs={{0,9},{1,10},{2,11},{3,12},{4,13},{5,14},{6,15},{7,0},{8,1},{9,2},... | collective-permute-start | bytes 129032 | tf_op jit(solution)/shard_map/ppermute | solution.py:16
  83.5 5.1 %collective-permute-start.7 = (bf16[1,6,3584]{2,1,0:T(8,128)(2,1)S(1)}, bf16[1,6,3584]{2,1,0:T(8,128)(2,1)S(1)}, u32[]{:S(2)}, u32[]{:S(2)}) collective-permute-start(bf16[1,6,3584]{2,1,0:T(8,128)(2,1)S(1)} %get-tuple-element.12), channel_id=1, source_target_pairs={{0,8},{1,9},{2,10},{3,11},{4,12},{5,13},{6,14},{7,15},{8,0},{9,1},... | collective-permute-start | bytes 129032 | tf_op jit(solution)/shard_map/ppermute | solution.py:16
  88.6 5.0 %collective-permute-start.8 = (bf16[1,6,3584]{2,1,0:T(8,128)(2,1)S(1)}, bf16[1,6,3584]{2,1,0:T(8,128)(2,1)S(1)}, u32[]{:S(2)}, u32[]{:S(2)}) collective-permute-start(bf16[1,6,3584]{2,1,0:T(8,128)(2,1)S(1)} %get-tuple-element.11), channel_id=1, source_target_pairs={{0,7},{1,8},{2,9},{3,10},{4,11},{5,12},{6,13},{7,14},{8,15},{9,0},... | collective-permute-start | bytes 129032 | tf_op jit(solution)/shard_map/ppermute | solution.py:16
  93.6 7.7 %collective-permute-start.9 = (bf16[1,6,3584]{2,1,0:T(8,128)(2,1)S(1)}, bf16[1,6,3584]{2,1,0:T(8,128)(2,1)S(1)}, u32[]{:S(2)}, u32[]{:S(2)}) collective-permute-start(bf16[1,6,3584]{2,1,0:T(8,128)(2,1)S(1)} %get-tuple-element.10), channel_id=1, source_target_pairs={{0,6},{1,7},{2,8},{3,9},{4,10},{5,11},{6,12},{7,13},{8,14},{9,15},... | collective-permute-start | bytes 129032 | tf_op jit(solution)/shard_map/ppermute | solution.py:16
  101.4 5.4 %collective-permute-start.10 = (bf16[1,6,3584]{2,1,0:T(8,128)(2,1)S(1)}, bf16[1,6,3584]{2,1,0:T(8,128)(2,1)S(1)}, u32[]{:S(2)}, u32[]{:S(2)}) collective-permute-start(bf16[1,6,3584]{2,1,0:T(8,128)(2,1)S(1)} %get-tuple-element.9), channel_id=1, source_target_pairs={{0,5},{1,6},{2,7},{3,8},{4,9},{5,10},{6,11},{7,12},{8,13},{9,14},{... | collective-permute-start | bytes 129032 | tf_op jit(solution)/shard_map/ppermute | solution.py:16
  111.1 5.7 %copy-start = (bf16[1,3584,512]{2,1,0:T(8,128)(2,1)S(1)}, bf16[1,3584,512]{2,1,0:T(8,128)(2,1)}, u32[]{:S(2)}) copy-start(bf16[1,3584,512]{2,1,0:T(8,128)(2,1)} %param.13) | copy-start | bytes 11010052
  116.8 2.0 %copy-start.1 = (bf16[1,3584,512]{2,1,0:T(8,128)(2,1)S(1)}, bf16[1,3584,512]{2,1,0:T(8,128)(2,1)}, u32[]{:S(2)}) copy-start(bf16[1,3584,512]{2,1,0:T(8,128)(2,1)} %param.14) | copy-start | bytes 11010052
  118.8 9.4 %copy-start.3 = (u32[32]{0:T(128)S(1)}, u32[32]{0:T(128)}, u32[]{:S(2)}) copy-start(u32[32]{0:T(128)} %constant.68) | copy-start | bytes 388
  121.2 29.3 %all-to-all-start.1 = ((bf16[16,6,3584]{2,1,0:T(8,128)(2,1)}), bf16[16,6,3584]{2,1,0:T(8,128)(2,1)S(1)}, u32[]{:S(2)}, u32[]{:S(2)}) async-start(bf16[16,6,3584]{2,1,0:T(8,128)(2,1)} %reshape.109), calls=%async_computation.1 | async-start | bytes 1835008 | tf_op jit(solution)/shard_map/all_to_all | solution.py:100
